TPU v7x, 128 devices: a whole 4x4x4 slice. The times are simulated.
128 devices in a mesh: tx: 8 (over y, core), ty: 16 (over z, x).
Axes of the slice: x: 4, y: 4, z: 4, core: 2. Of those that a mesh axis runs over, the one named last changes fastest.
Arguments:
- increment: float32 [32, 640, 3072], P(None, 'ty', 'tx'), may hold values from -6 to 6
- vert_rate: float32 [2, 16], replicated, may hold values from 0.05 to 0.8
- zonal_rate: float32 [16, 32], replicated, may hold values from 0.003 to 0.12
- merid_rate: float32 [16, 32], replicated, may hold values from 0.02 to 0.12
- lat_band: int32 [640], replicated, may hold values from 0 to 15, never falling along the last dimension, each value on 1 to 80 neighbouring positions
- slab_owner: int32 [32], replicated, may hold values from 0 to 7, as said below
Outputs:
- covariance_product: float32 [32, 640, 3072], P(None, 'ty', 'tx')
- filtered_slabs: float32 [64, 640, 3072], P('tx', 'ty')
Inputs may be any that keep to these rules, and one draw needn't show every extreme that they name: lat_band never falls along y and every band appears. `slab_owner`: each index of tx owns at most 8 slabs, and some index owns exactly 8.
All inputs are finite; a program needn't handle non-finite values.
Results may differ from a plain program's by a relative error of at most 0.0003.
Values sent between devices are 32-bit elements; how exact they have to be, the bound alone decides.
A program may use at most 128 MiB of HBM per device.

v0:
```python
import jax
import jax.numpy as jnp
from jax import lax
from jax.sharding import PartitionSpec as P

LEV = 16
VAR = 2
NBANDS = 16
HIGHEST_PRECISION = lax.Precision.HIGHEST


def chain_matrices(log_decay, gains):
    length = log_decay.shape[-1]
    inclusive = jnp.cumsum(log_decay, axis=-1)
    exclusive = inclusive - log_decay
    index = jnp.arange(length)
    lower = index[:, None] >= index[None, :]
    upper = index[:, None] <= index[None, :]
    fdiff = inclusive[..., :, None] - inclusive[..., None, :]
    forward = jnp.where(lower, jnp.exp(jnp.where(lower, fdiff, 0.0)), 0.0) * gains[..., None, :]
    bdiff = exclusive[..., None, :] - exclusive[..., :, None]
    backward = jnp.where(upper, jnp.exp(jnp.where(upper, bdiff, 0.0)), 0.0) * gains[..., None, :]
    return (forward, backward)


def gain_of(rates):
    return jnp.sqrt(rates * (2.0 - rates))


def vertical_apply(vert_matrix, values):
    slabs, tile_rows, tile_cols = values.shape
    stacked = values.reshape(VAR, LEV, tile_rows * tile_cols)
    result = jnp.einsum("vlk,vkn->vln", vert_matrix, stacked, precision=HIGHEST_PRECISION)
    return result.reshape(slabs, tile_rows, tile_cols)


def affine_combine(first, second):
    return (first[0] * second[0], second[0] * first[1] + second[1])


def carry_blocks(block_decay, ends):
    scale = jnp.broadcast_to(block_decay, ends.shape)
    inclusive = lax.associative_scan(affine_combine, (scale, ends), axis=2)[1]
    return jnp.concatenate([jnp.zeros_like(inclusive[..., :1]), inclusive[..., :-1]], axis=2)


def carry_row_blocks(block_decay, ends):
    scale = jnp.broadcast_to(block_decay[..., None], ends.shape)
    inclusive = lax.associative_scan(affine_combine, (scale, ends), axis=1)[1]
    return jnp.concatenate([jnp.zeros_like(inclusive[:, :1]), inclusive[:, :-1]], axis=1)


def zonal_filter(values, rates):
    capacity, tile_rows, width = values.shape
    blocks = width // 128
    shaped = values.reshape(capacity, tile_rows, blocks, 128)
    log_decay = jnp.log1p(-rates)[:, :, None, None]
    gains = gain_of(rates)[:, :, None, None]
    offset = jnp.arange(128, dtype=jnp.float32)
    rising = jnp.exp(offset * log_decay)
    falling = jnp.exp(-offset * log_decay)
    index = jnp.arange(128)
    upto = (index[:, None] <= index[None, :]).astype(jnp.float32)
    block_decay = jnp.exp(128.0 * log_decay[..., 0])
    partial_value = jnp.einsum(
        "crbj,ji->crbi", shaped * gains * falling, upto, precision=HIGHEST_PRECISION
    )
    local = rising * partial_value
    entering = carry_blocks(block_decay, local[..., 127])
    forward = local + rising * jnp.exp(log_decay) * entering[..., None]
    partial_back = jnp.einsum(
        "crbj,ij->crbi", forward * gains * rising, upto, precision=HIGHEST_PRECISION
    )
    local_back = falling * partial_back
    from_above = jnp.flip(carry_blocks(block_decay, jnp.flip(local_back[..., 0], 2)), 2)
    backward = local_back + jnp.exp((128.0 - offset) * log_decay) * from_above[..., None]
    return backward.reshape(capacity, tile_rows, width)


def column_filter(values, rates):
    capacity, rows, cols = values.shape
    block = min(rows, 128)
    blocks = rows // block
    shaped = values.reshape(capacity, blocks, block, cols)
    log_decay = jnp.log1p(-rates).reshape(capacity, blocks, block)
    gains = gain_of(rates).reshape(capacity, blocks, block)
    forward_mat, backward_mat = chain_matrices(log_decay, gains)
    local = jnp.einsum("cbij,cbjx->cbix", forward_mat, shaped, precision=HIGHEST_PRECISION)
    inclusive = jnp.cumsum(log_decay, axis=2)
    whole_decay = inclusive[:, :, -1]
    block_decay = jnp.exp(whole_decay)
    entering = carry_row_blocks(block_decay, local[:, :, -1, :])
    forward = local + jnp.exp(inclusive)[..., None] * entering[:, :, None, :]
    local_back = jnp.einsum("cbij,cbjx->cbix", backward_mat, forward, precision=HIGHEST_PRECISION)
    from_above = jnp.flip(
        carry_row_blocks(jnp.flip(block_decay, 1), jnp.flip(local_back[:, :, 0, :], 1)), 1
    )
    exclusive = inclusive - log_decay
    tail = jnp.exp(whole_decay[..., None] - exclusive)
    backward = local_back + tail[..., None] * from_above[:, :, None, :]
    return backward.reshape(capacity, rows, cols)


def shards(increment, vert_rate, zonal_rate, merid_rate, lat_band, slab_owner):
    slabs, tile_rows, tile_cols = increment.shape
    groups_x = lax.axis_size("tx")
    capacity = 2 * slabs // groups_x
    index_x = lax.axis_index("tx")
    index_y = lax.axis_index("ty")
    vert_fwd, vert_bwd = chain_matrices(jnp.log1p(-vert_rate), gain_of(vert_rate))
    vert_matrix = jnp.einsum("vij,vjk->vik", vert_bwd, vert_fwd, precision=HIGHEST_PRECISION)
    vertical = vertical_apply(vert_matrix, increment)
    slab_index = jnp.arange(slabs, dtype=jnp.int32)
    same = slab_owner[:, None] == slab_owner[None, :]
    earlier = slab_index[None, :] < slab_index[:, None]
    slot = jnp.sum(jnp.logical_and(same, earlier), axis=1)
    target = slab_owner * capacity + slot
    slot_rows = jnp.arange(groups_x * capacity, dtype=jnp.int32)
    matches = target[None, :] == slot_rows[:, None]
    source = jnp.sum(jnp.where(matches, slab_index[None, :], 0), axis=1)
    filled = jnp.any(matches, axis=1).astype(jnp.float32)
    outgoing = jnp.take(vertical, source, axis=0) * filled[:, None, None]
    lines = lax.all_to_all(outgoing, "tx", split_axis=0, concat_axis=2, tiled=True)
    mine = lax.dynamic_slice_in_dim(source, index_x * capacity, capacity)
    mine_filled = lax.dynamic_slice_in_dim(filled, index_x * capacity, capacity)
    slab_onehot = (mine[:, None] == slab_index[None, :]).astype(jnp.float32) * mine_filled[:, None]
    band_onehot = (lat_band[:, None] == jnp.arange(NBANDS)[None, :]).astype(jnp.float32)
    row_onehot = lax.dynamic_slice_in_dim(band_onehot, index_y * tile_rows, tile_rows)
    zonal_table = jnp.dot(slab_onehot, zonal_rate.T, precision=HIGHEST_PRECISION)
    merid_table = jnp.dot(slab_onehot, merid_rate.T, precision=HIGHEST_PRECISION)
    zonal_rows = jnp.dot(zonal_table, row_onehot.T, precision=HIGHEST_PRECISION)
    zonal = zonal_filter(lines, zonal_rows)
    columns = lax.all_to_all(zonal, "ty", split_axis=2, concat_axis=1, tiled=True)
    merid_full = jnp.dot(merid_table, band_onehot.T, precision=HIGHEST_PRECISION)
    smoothed_columns = column_filter(columns, merid_full)
    smoothed = lax.all_to_all(smoothed_columns, "ty", split_axis=1, concat_axis=2, tiled=True)
    returned = lax.all_to_all(smoothed, "tx", split_axis=2, concat_axis=0, tiled=True)
    gathered = jnp.take(returned, target, axis=0)
    covariance_product = vertical_apply(vert_matrix, gathered)
    return (covariance_product, smoothed)


def solution(mesh):
    return jax.shard_map(
        shards,
        mesh=mesh,
        in_specs=(P(None, "ty", "tx"), P(), P(), P(), P(), P()),
        out_specs=(P(None, "ty", "tx"), P("tx", "ty", None)),
        check_vma=False,
    )
```

profile of v0, /device:TPU:1, one launch (start us, length us, event | category | flops | bytes accessed | tf_op | source)
XLA Modules:
  0.0 487.3 jit_solution(7366706735983362756)
XLA Ops:
  0.6 0.9 convert_reduce_fusion
  1.6 0.7 compare_and_fusion.1
  2.5 0.7 negate_log-plus-one_fusion.1
  3.1 0.2 reduce_window_sum.24
  3.3 0.7 fusion.108
  4.0 1.7 reshape.152
  5.8 0.2 fusion.61
  6.0 1.8 fusion.118
  7.8 0.4 copy.268
  8.2 2.7 gather_fusion
  10.9 4.4 select_multiply_fusion
  15.3 6.3 %all-to-all-start = ((f32[64,40,384]{2,1,0:T(8,128)}), f32[64,40,384]{2,1,0:T(8,128)}, u32[]{:S(2)}, u32[]{:S(2)}) async-start(f32[64,40,384]{2,1,0:T(8,128)} %select_multiply_fusion), calls=%async_computation | async-start | bytes 7864320 | tf_op jit(solution)/shard_map/all_to_all | solution.py:123
  21.8 0.2 fusion.87
  22.0 0.2 iota_compare_fusion
  22.2 0.2 fusion.111
  22.4 0.2 multiply_exponential_fusion
  22.5 45.0 %all-to-all-done = f32[64,40,384]{2,1,0:T(8,128)} async-done(((f32[64,40,384]{2,1,0:T(8,128)}), f32[64,40,384]{2,1,0:T(8,128)}, u32[]{:S(2)}, u32[]{:S(2)}) %all-to-all-start) | async-done | bytes 3932192 | tf_op jit(solution)/shard_map/all_to_all | solution.py:123
  67.6 6.3 %copy.226 = f32[8,40,8,384]{3,2,1,0:T(8,128)} copy(f32[8,40,8,384]{3,1,0,2:T(8,128)} %bitcast.5) | data formatting | bytes 7864320 | tf_op jit(solution)/shard_map/all_to_all | solution.py:123
  73.9 4.7 reshape.154
  78.5 4.4 fusion.22
  82.9 1.9 copy-done.2
  84.8 2.9 slice.372
  87.8 3.0 copy.227
  91.9 0.1 copy.266
  92.1 5.7 %fusion.31 = f32[8,40,24,128]{3,2,1,0:T(8,128)} fusion(f32[8,40,24,128]{3,2,1,0:T(8,128)} %copy-done.2, f32[8,40,24]{2,1,0:T(8,128)S(1)} %concatenate.46.clone, f32[8,40,128]{2,1,0:T(8,128)S(1)} %get-tuple-element.29, f32[8,40]{1,0:T(8,128)S(1)} %get-tuple-element.37, f32[8,40,128]{2,1,0:T(8,128)S(1)} %get-tuple-element.30, ...), kind=kOutput, calls=%fused_computation.34 | convolution fusion | flops 1514881024 | bytes 8387840 | tf_op jit(solution)/shard_map/crbj,ij->crbi/dot_general | solution.py:71
  97.8 3.0 copy.231
  102.1 4.1 multiply_add_fusion.1
  106.2 7.9 %copy.260 = f32[8,40,24,128]{1,0,3,2:T(8,128)} copy(f32[8,40,24,128]{3,2,1,0:T(8,128)} %multiply_add_fusion.1) | data formatting | bytes 7864320 | tf_op jit(solution)/shard_map/reshape | solution.py:77
  114.1 17.2 %reshape.179 = f32[16,1,61440]{2,1,0:T(1,128)} reshape(f32[3072,8,40]{2,1,0:T(8,128)} %bitcast.74) | data formatting | bytes 7864320
  131.2 8.2 %all-to-all-start.1 = ((f32[16,1,61440]{2,1,0:T(1,128)}), f32[16,1,61440]{2,1,0:T(1,128)}, u32[]{:S(2)}, u32[]{:S(2)}) async-start(f32[16,1,61440]{2,1,0:T(1,128)} %reshape.179), calls=%async_computation.1 | async-start | bytes 7864320 | tf_op jit(solution)/shard_map/all_to_all | solution.py:133
  139.4 0.2 fusion.89
  139.6 0.4 fusion.100
  140.0 1.4 reduce_window_sum.25
  141.6 0.1 copy.240
  142.1 0.1 copy.244
  143.1 0.2 slice_reduce_fusion.1
  143.3 0.2 slice_reduce_fusion
  143.5 53.7 %all-to-all-done.1 = f32[16,1,61440]{2,1,0:T(1,128)} async-done(((f32[16,1,61440]{2,1,0:T(1,128)}), f32[16,1,61440]{2,1,0:T(1,128)}, u32[]{:S(2)}, u32[]{:S(2)}) %all-to-all-start.1) | async-done | bytes 3932192 | tf_op jit(solution)/shard_map/all_to_all | solution.py:133
  197.2 0.5 broadcast.205
  197.7 13.6 %reduce.4 = f32[16,61440]{1,0:T(8,128)} reduce(f32[16,1,61440]{2,1,0:T(1,128)} %all-to-all-done.1, f32[]{:T(128)} %broadcast.205), dimensions={1}, to_apply=%all_to_all.51.reduce_sub_computation | reduce | bytes 7864324 | tf_op jit(solution)/shard_map/all_to_all | solution.py:133
  211.4 18.7 %reshape.180 = f32[3072,8,40]{2,1,0:T(8,128)} reshape(f32[16,61440]{1,0:T(8,128)} %reduce.4) | data formatting | bytes 7864320
  230.0 10.9 %copy.236 = f32[8,40,16,192]{3,1,2,0:T(8,128)} copy(f32[8,40,16,192]{1,0,3,2:T(8,128)} %bitcast.75) | data formatting | bytes 7864320 | tf_op jit(solution)/shard_map/all_to_all | solution.py:133
  240.9 11.2 %fusion.11 = f32[8,5,128,192]{2,3,1,0:T(8,128)S(1)} fusion(f32[8,5,128,192]{3,2,1,0:T(8,128)} %bitcast.82, f32[8,5,128]{2,1,0:T(8,128)S(1)} %copy.224, f32[8,5,128]{2,1,0:T(8,128)S(1)} %copy.223, pred[128,128]{1,0:T(8,128)(4,1)S(1)} %iota_compare_fusion.1), kind=kOutput, calls=%fused_computation.16 | convolution fusion | flops 1512570880 | bytes 7921664 | tf_op jit(solution)/shard_map/cbij,cbjx->cbix/dot_general | solution.py:88
  252.1 1.9 copy-done.3
  254.0 2.9 slice.398
  257.0 3.5 copy.239
  260.8 9.1 %fusion = f32[8,5,128,192]{2,3,1,0:T(8,128)} fusion(f32[8,5,128,192]{2,3,1,0:T(8,128)} %copy-done.3, f32[8,5,192]{2,1,0:T(8,128)S(1)} %concatenate.53.clone, f32[8,5,128]{2,1,0:T(8,128)S(1)} %copy.238, f32[8,5,128]{2,1,0:T(8,128)S(1)} %copy.223, f32[8,5,128]{2,1,0:T(8,128)S(1)} %copy.221, pred[128,128]{1,0:T(8,128)(4,1)S(1)} %iota_compare_fusion.2), kind=kOutput, calls=%fused_computation.3 | convolution fusion | flops 1514536960 | bytes 7972864 | tf_op jit(solution)/shard_map/cbij,cbjx->cbix/dot_general | solution.py:94
  269.9 3.5 copy.247
  273.8 4.1 multiply_add_fusion
  277.9 5.9 %copy.262 = f32[8,5,128,192]{3,0,2,1:T(8,128)} copy(f32[8,5,128,192]{2,3,1,0:T(8,128)} %multiply_add_fusion) | data formatting | bytes 7864320 | tf_op jit(solution)/shard_map/reshape | solution.py:101
  283.8 65.7 %all_to_all.66 = f32[8,640,192]{2,0,1:T(8,128)S(1)} all-to-all(f32[8,640,192]{2,0,1:T(8,128)} %bitcast.80), channel_id=1, replica_groups=mesh['tx'=8,'ty'=16] {'ty'}, dimensions={1} | all-to-all | bytes 7864320 | tf_op jit(solution)/shard_map/all_to_all | solution.py:136
  349.5 5.3 %copy.254 = f32[8,40,16,192]{3,2,1,0:T(8,128)} copy(f32[8,40,16,192]{3,0,1,2:T(8,128)S(1)} %bitcast.81) | data formatting | bytes 7864320 | tf_op jit(solution)/shard_map/all_to_all | solution.py:136
  354.8 5.8 %all_to_all.57 = f32[8,40,3072]{2,1,0:T(8,128)} reshape(f32[8,40,16,192]{3,2,1,0:T(8,128)} %copy.254) | data formatting | bytes 7864320 | tf_op jit(solution)/shard_map/all_to_all | solution.py:136
  360.6 8.8 %copy.255 = f32[8,40,3072]{1,0,2:T(8,128)} copy(f32[8,40,3072]{2,1,0:T(8,128)} %all_to_all.57) | data formatting | bytes 7864320 | tf_op jit(solution)/shard_map/all_to_all | solution.py:136
  369.5 14.8 %reshape.181 = f32[8,1,122880]{2,1,0:T(1,128)} reshape(f32[3072,8,40]{2,1,0:T(8,128)} %bitcast.77) | data formatting | bytes 7864320
  384.3 7.9 %all-to-all-start.3 = ((f32[8,1,122880]{2,1,0:T(1,128)}), f32[8,1,122880]{2,1,0:T(1,128)}, u32[]{:S(2)}, u32[]{:S(2)}) async-start(f32[8,1,122880]{2,1,0:T(1,128)} %reshape.181), calls=%async_computation.3 | async-start | bytes 7864320 | tf_op jit(solution)/shard_map/all_to_all | solution.py:137
  392.2 45.8 %all-to-all-done.3 = f32[8,1,122880]{2,1,0:T(1,128)} async-done(((f32[8,1,122880]{2,1,0:T(1,128)}), f32[8,1,122880]{2,1,0:T(1,128)}, u32[]{:S(2)}, u32[]{:S(2)}) %all-to-all-start.3) | async-done | bytes 3932192 | tf_op jit(solution)/shard_map/all_to_all | solution.py:137
  438.1 13.9 %reduce.5 = f32[8,122880]{1,0:T(8,128)} reduce(f32[8,1,122880]{2,1,0:T(1,128)} %all-to-all-done.3, f32[]{:T(128)} %broadcast.205), dimensions={1}, to_apply=%all_to_all.58.reduce_sub_computation | reduce | bytes 7864324 | tf_op jit(solution)/shard_map/all_to_all | solution.py:137
  452.0 16.8 %reshape.182 = f32[3072,8,40]{2,1,0:T(8,128)} reshape(f32[8,122880]{1,0:T(8,128)} %reduce.5) | data formatting | bytes 7864320
  468.7 9.1 %copy.257 = f32[8,8,40,384]{3,2,1,0:T(8,128)} copy(f32[8,8,40,384]{2,1,3,0:T(8,128)} %bitcast.76) | data formatting | bytes 7864320 | tf_op jit(solution)/shard_map/all_to_all | solution.py:137
  477.8 4.1 gather_fusion.1
  481.9 1.7 gather.12
  483.6 1.8 fusion.25
  485.4 1.6 copy.269
  (147 shorter events, 4.6 us)
Async XLA Ops:
  0.6 21.2 %copy-start = (f32[16,32]{1,0:T(8,128)S(1)}, f32[16,32]{1,0:T(8,128)}, u32[]{:S(2)}) copy-start(f32[16,32]{1,0:T(8,128)} %param.8) | copy-start | bytes 6148
  15.3 6.7 %copy-start.4 = (s32[640]{0:T(1024)S(1)}, s32[640]{0:T(1024)}, u32[]{:S(2)}) copy-start(s32[640]{0:T(1024)} %param.10) | copy-start | bytes 7684
  15.3 52.2 %all-to-all-start = ((f32[64,40,384]{2,1,0:T(8,128)}), f32[64,40,384]{2,1,0:T(8,128)}, u32[]{:S(2)}, u32[]{:S(2)}) async-start(f32[64,40,384]{2,1,0:T(8,128)} %select_multiply_fusion), calls=%async_computation | async-start | bytes 7864320 | tf_op jit(solution)/shard_map/all_to_all | solution.py:123
  82.9 1.9 copy-start.2
  131.2 8.2 %copy-start.5 = (f32[16,32]{1,0:T(8,128)S(1)}, f32[16,32]{1,0:T(8,128)}, u32[]{:S(2)}) copy-start(f32[16,32]{1,0:T(8,128)} %param.9) | copy-start | bytes 6148
  131.2 66.0 %all-to-all-start.1 = ((f32[16,1,61440]{2,1,0:T(1,128)}), f32[16,1,61440]{2,1,0:T(1,128)}, u32[]{:S(2)}, u32[]{:S(2)}) async-start(f32[16,1,61440]{2,1,0:T(1,128)} %reshape.179), calls=%async_computation.1 | async-start | bytes 7864320 | tf_op jit(solution)/shard_map/all_to_all | solution.py:133
  252.1 1.9 copy-start.3
  384.3 53.8 %all-to-all-start.3 = ((f32[8,1,122880]{2,1,0:T(1,128)}), f32[8,1,122880]{2,1,0:T(1,128)}, u32[]{:S(2)}, u32[]{:S(2)}) async-start(f32[8,1,122880]{2,1,0:T(1,128)} %reshape.181), calls=%async_computation.3 | async-start | bytes 7864320 | tf_op jit(solution)/shard_map/all_to_all | solution.py:137
  481.9 5.2 %copy-start.1 = (f32[16,32]{1,0:T(8,128)S(1)}, f32[16,32]{1,0:T(8,128)}, u32[]{:S(2)}) copy-start(f32[16,32]{1,0:T(8,128)} %param.8) | copy-start | bytes 6148
where the time goes:
time: 493 us; the launch traced here: 487 us
  local copies, waits for them, and re-layouts  172 us (35%)
  waiting for transfers between devices  145 us (29%)
  blocking collectives  65.7 us (13%)
  other arithmetic  46.2 us (9%)
  matrix products  35 us (7%)
  starting transfers between devices  22.4 us (5%)
    unnamed x24, local copies, waits for them, and re-layouts  73.5 us
    all_to_all x1, blocking collectives, shards(): lax.all_to_all(smoothed_columns, 'ty', split_axis=1, concat_axis=2, tiled...  65.7 us
    all_to_all x1, waiting for transfers between devices, shards(): lax.all_to_all(zonal, 'ty', split_axis=2, concat_axis=1, tiled=True)  53.7 us
    all_to_all x1, waiting for transfers between devices, shards(): lax.all_to_all(smoothed, 'tx', split_axis=2, concat_axis=0, tiled=True)  45.8 us
    all_to_all x1, waiting for transfers between devices, shards(): lax.all_to_all(outgoing, 'tx', split_axis=0, concat_axis=2, tiled=True)  45 us
    all_to_all x3, local copies, waits for them, and re-layouts, shards(): lax.all_to_all(smoothed_columns, 'ty', split_axis=1, concat_axis=2, tiled...  20 us
    all_to_all x1, other arithmetic, shards(): lax.all_to_all(smoothed, 'tx', split_axis=2, concat_axis=0, tiled=True)  13.9 us
    all_to_all x1, other arithmetic, shards(): lax.all_to_all(zonal, 'ty', split_axis=2, concat_axis=1, tiled=True)  13.6 us
  transfers between devices with their start and end apart: 3, of which 3 were waited for; matrix products, arithmetic and copies ran while one was open for 1% of the time, Pallas kernels for 0%

commit v1 on v0

--- a/solution.py
+++ b/solution.py
@@ -134,7 +134,10 @@
     merid_full = jnp.dot(merid_table, band_onehot.T, precision=HIGHEST_PRECISION)
     smoothed_columns = column_filter(columns, merid_full)
     smoothed = lax.all_to_all(smoothed_columns, "ty", split_axis=1, concat_axis=2, tiled=True)
-    returned = lax.all_to_all(smoothed, "tx", split_axis=2, concat_axis=0, tiled=True)
+    returned = jnp.concatenate(
+        lax.all_to_all(jnp.stack(jnp.split(smoothed, lax.axis_size("tx"), axis=2)), "tx", 0, 0),
+        axis=0,
+    )
     gathered = jnp.take(returned, target, axis=0)
     covariance_product = vertical_apply(vert_matrix, gathered)
     return (covariance_product, smoothed)

time: 493 us -> 444 us (0.901)
  local copies, waits for them, and re-layouts: 172 us -> 137 us
  other arithmetic: 46.2 us -> 32.3 us
    unnamed x24 -> x29, local copies, waits for them, and re-layouts: 73.5 us -> 54.9 us
    all_to_all x1 -> x0, other arithmetic: 13.9 us -> none  [shards(): lax.all_to_all(smoothed, 'tx', split_axis=2, concat_axis=0, tiled=True)]
    all_to_all x1 -> x0, local copies, waits for them, and re-layouts: 9.1 us -> none  [shards(): lax.all_to_all(smoothed, 'tx', split_axis=2, concat_axis=0, tiled=True)]
    all_to_all x3 -> x2, local copies, waits for them, and re-layouts: 20 us -> 11.1 us  [shards(): lax.all_to_all(smoothed_columns, 'ty', split_axis=1, concat_axis=2, tiled...]
where the time goes in v1:
time: 444 us; the launch traced here: 439 us
  waiting for transfers between devices  145 us (33%)
  local copies, waits for them, and re-layouts  137 us (31%)
  blocking collectives  65.7 us (15%)
  matrix products  35.1 us (8%)
  other arithmetic  32.3 us (7%)
  starting transfers between devices  22.5 us (5%)
    all_to_all x1, blocking collectives, shards(): lax.all_to_all(smoothed_columns, 'ty', split_axis=1, concat_axis=2, tiled...  65.7 us
    unnamed x29, local copies, waits for them, and re-layouts  54.9 us
    all_to_all x1, waiting for transfers between devices, shards(): lax.all_to_all(zonal, 'ty', split_axis=2, concat_axis=1, tiled=True)  53.7 us
    all_to_all x1, waiting for transfers between devices, shards(): lax.all_to_all(jnp.stack(jnp.split(smoothed, lax.axis_size('tx'), axis=2)...  45.8 us
    all_to_all x1, waiting for transfers between devices, shards(): lax.all_to_all(outgoing, 'tx', split_axis=0, concat_axis=2, tiled=True)  45 us
    all_to_all x1, other arithmetic, shards(): lax.all_to_all(zonal, 'ty', split_axis=2, concat_axis=1, tiled=True)  13.6 us
    all_to_all x2, local copies, waits for them, and re-layouts, shards(): lax.all_to_all(zonal, 'ty', split_axis=2, concat_axis=1, tiled=True)  11.4 us
    dot_general x1, matrix products, column_filter(): jnp.einsum('cbij,cbjx->cbix', forward_mat, shaped, precision=HIGHEST_PREC...  11.2 us
  transfers between devices with their start and end apart: 3, of which 3 were waited for; matrix products, arithmetic and copies ran while one was open for 1% of the time, Pallas kernels for 0%

profile of v1, /device:TPU:1, one launch (start us, length us, event | category | flops | bytes accessed | tf_op | source)
XLA Modules:
  0.0 438.8 jit_solution(17386085900638693960)
XLA Ops:
  0.6 0.9 convert_reduce_fusion
  1.6 0.7 compare_and_fusion.1
  2.5 0.7 negate_log-plus-one_fusion.1
  3.1 0.2 reduce_window_sum.24
  3.3 0.7 fusion.116
  4.0 1.7 reshape.155
  5.8 0.2 fusion.69
  6.0 1.8 fusion.126
  7.8 0.4 copy.250
  8.2 2.7 gather_fusion
  10.9 4.4 %select_multiply_fusion = f32[64,40,384]{2,1,0:T(8,128)} fusion(f32[64,40,384]{2,1,0:T(8,128)} %gather_fusion, f32[64]{0:T(128)S(1)} %convert_element_type.14, pred[64]{0:T(512)(128)(4,1)S(1)} %compare_and_fusion), kind=kLoop, calls=%fused_computation.15 | loop fusion | flops 1966080 | bytes 7864640 | tf_op jit(solution)/shard_map/mul | solution.py:122
  15.3 6.7 %all-to-all-start = ((f32[64,40,384]{2,1,0:T(8,128)}), f32[64,40,384]{2,1,0:T(8,128)}, u32[]{:S(2)}, u32[]{:S(2)}) async-start(f32[64,40,384]{2,1,0:T(8,128)} %select_multiply_fusion), calls=%async_computation | async-start | bytes 7864320 | tf_op jit(solution)/shard_map/all_to_all | solution.py:123
  22.2 0.2 fusion.95
  22.4 0.2 iota_compare_fusion
  22.5 0.2 fusion.119
  22.7 0.2 multiply_exponential_fusion
  22.9 45.0 %all-to-all-done = f32[64,40,384]{2,1,0:T(8,128)} async-done(((f32[64,40,384]{2,1,0:T(8,128)}), f32[64,40,384]{2,1,0:T(8,128)}, u32[]{:S(2)}, u32[]{:S(2)}) %all-to-all-start) | async-done | bytes 3932192 | tf_op jit(solution)/shard_map/all_to_all | solution.py:123
  67.9 6.3 %copy.213 = f32[8,40,8,384]{3,2,1,0:T(8,128)} copy(f32[8,40,8,384]{3,1,0,2:T(8,128)} %bitcast.5) | data formatting | bytes 7864320 | tf_op jit(solution)/shard_map/all_to_all | solution.py:123
  74.2 4.7 %reshape.157 = f32[8,40,24,128]{3,2,1,0:T(8,128)} reshape(f32[8,40,8,384]{3,2,1,0:T(8,128)} %copy.213) | data formatting | bytes 7864320 | tf_op jit(solution)/shard_map/reshape | solution.py:56
  78.9 4.4 fusion.22
  83.3 1.9 copy-done.2
  85.2 2.9 slice.372
  88.1 3.0 copy.214
  92.4 5.7 %fusion.31 = f32[8,40,24,128]{3,2,1,0:T(8,128)} fusion(f32[8,40,24,128]{3,2,1,0:T(8,128)} %copy-done.2, f32[8,40,24]{2,1,0:T(8,128)S(1)} %concatenate.46.clone, f32[8,40,128]{2,1,0:T(8,128)S(1)} %get-tuple-element.29, f32[8,40]{1,0:T(8,128)S(1)} %get-tuple-element.37, f32[8,40,128]{2,1,0:T(8,128)S(1)} %get-tuple-element.30, ...), kind=kOutput, calls=%fused_computation.34 | convolution fusion | flops 1514881024 | bytes 8387840 | tf_op jit(solution)/shard_map/crbj,ij->crbi/dot_general | solution.py:71
  98.1 3.0 copy.218
  102.4 4.1 multiply_add_fusion.1
  106.5 7.9 %copy.244 = f32[8,40,24,128]{1,0,3,2:T(8,128)} copy(f32[8,40,24,128]{3,2,1,0:T(8,128)} %multiply_add_fusion.1) | data formatting | bytes 7864320 | tf_op jit(solution)/shard_map/reshape | solution.py:77
  114.4 17.2 %reshape.183 = f32[16,1,61440]{2,1,0:T(1,128)} reshape(f32[3072,8,40]{2,1,0:T(8,128)} %bitcast.100) | data formatting | bytes 7864320
  131.5 8.0 %all-to-all-start.1 = ((f32[16,1,61440]{2,1,0:T(1,128)}), f32[16,1,61440]{2,1,0:T(1,128)}, u32[]{:S(2)}, u32[]{:S(2)}) async-start(f32[16,1,61440]{2,1,0:T(1,128)} %reshape.183), calls=%async_computation.1 | async-start | bytes 7864320 | tf_op jit(solution)/shard_map/all_to_all | solution.py:133
  139.5 0.2 fusion.97
  139.7 0.4 fusion.108
  140.1 1.4 reduce_window_sum.25
  143.2 0.2 slice_reduce_fusion.1
  143.4 0.2 slice_reduce_fusion
  143.6 53.7 %all-to-all-done.1 = f32[16,1,61440]{2,1,0:T(1,128)} async-done(((f32[16,1,61440]{2,1,0:T(1,128)}), f32[16,1,61440]{2,1,0:T(1,128)}, u32[]{:S(2)}, u32[]{:S(2)}) %all-to-all-start.1) | async-done | bytes 3932192 | tf_op jit(solution)/shard_map/all_to_all | solution.py:133
  197.3 0.5 broadcast.205
  197.8 13.6 %reduce.4 = f32[16,61440]{1,0:T(8,128)} reduce(f32[16,1,61440]{2,1,0:T(1,128)} %all-to-all-done.1, f32[]{:T(128)} %broadcast.205), dimensions={1}, to_apply=%all_to_all.41.reduce_sub_computation | reduce | bytes 7864324 | tf_op jit(solution)/shard_map/all_to_all | solution.py:133
  211.4 18.7 %reshape.184 = f32[3072,8,40]{2,1,0:T(8,128)} reshape(f32[16,61440]{1,0:T(8,128)} %reduce.4) | data formatting | bytes 7864320
  230.1 10.9 %copy.223 = f32[8,40,16,192]{3,1,2,0:T(8,128)} copy(f32[8,40,16,192]{1,0,3,2:T(8,128)} %bitcast.101) | data formatting | bytes 7864320 | tf_op jit(solution)/shard_map/all_to_all | solution.py:133
  241.0 11.2 %fusion.11 = f32[8,5,128,192]{2,3,1,0:T(8,128)S(1)} fusion(f32[8,5,128,192]{3,2,1,0:T(8,128)} %bitcast.106, f32[8,5,128]{2,1,0:T(8,128)S(1)} %copy.211, f32[8,5,128]{2,1,0:T(8,128)S(1)} %copy.210, pred[128,128]{1,0:T(8,128)(4,1)S(1)} %iota_compare_fusion.1), kind=kOutput, calls=%fused_computation.16 | convolution fusion | flops 1512570880 | bytes 7921664 | tf_op jit(solution)/shard_map/cbij,cbjx->cbix/dot_general | solution.py:88
  252.2 1.9 copy-done.3
  254.1 2.9 slice.398
  257.0 3.5 copy.226
  260.9 9.1 %fusion = f32[8,5,128,192]{2,3,1,0:T(8,128)} fusion(f32[8,5,128,192]{2,3,1,0:T(8,128)} %copy-done.3, f32[8,5,192]{2,1,0:T(8,128)S(1)} %concatenate.53.clone, f32[8,5,128]{2,1,0:T(8,128)S(1)} %copy.225, f32[8,5,128]{2,1,0:T(8,128)S(1)} %copy.210, f32[8,5,128]{2,1,0:T(8,128)S(1)} %copy.208, pred[128,128]{1,0:T(8,128)(4,1)S(1)} %iota_compare_fusion.2), kind=kOutput, calls=%fused_computation.3 | convolution fusion | flops 1514536960 | bytes 7972864 | tf_op jit(solution)/shard_map/cbij,cbjx->cbix/dot_general | solution.py:94
  270.0 3.5 copy.234
  273.9 4.1 multiply_add_fusion
  277.9 5.9 %copy.246 = f32[8,5,128,192]{3,0,2,1:T(8,128)} copy(f32[8,5,128,192]{2,3,1,0:T(8,128)} %multiply_add_fusion) | data formatting | bytes 7864320 | tf_op jit(solution)/shard_map/reshape | solution.py:101
  283.9 65.7 %all_to_all.53 = f32[8,640,192]{2,0,1:T(8,128)S(1)} all-to-all(f32[8,640,192]{2,0,1:T(8,128)} %bitcast.104), channel_id=1, replica_groups=mesh['tx'=8,'ty'=16] {'ty'}, dimensions={1} | all-to-all | bytes 7864320 | tf_op jit(solution)/shard_map/all_to_all | solution.py:136
  349.5 5.3 %copy.241 = f32[8,40,16,192]{3,2,1,0:T(8,128)} copy(f32[8,40,16,192]{3,0,1,2:T(8,128)S(1)} %bitcast.105) | data formatting | bytes 7864320 | tf_op jit(solution)/shard_map/all_to_all | solution.py:136
  354.9 5.8 %all_to_all.47 = f32[8,40,3072]{2,1,0:T(8,128)} reshape(f32[8,40,16,192]{3,2,1,0:T(8,128)} %copy.241) | data formatting | bytes 7864320 | tf_op jit(solution)/shard_map/all_to_all | solution.py:136
  360.7 1.8 fusion.57
  362.5 1.9 fusion.56
  364.4 1.8 fusion.55
  366.2 1.9 fusion.54
  368.1 1.8 fusion.53
  369.9 1.9 fusion.52
  371.8 1.8 fusion.51
  373.7 1.8 fusion.50
  375.5 7.9 %all-to-all-start.3 = ((f32[8,8,40,384]{3,2,1,0:T(8,128)}), f32[8,8,40,384]{3,2,1,0:T(8,128)}, u32[]{:S(2)}, u32[]{:S(2)}) async-start(f32[8,8,40,384]{3,2,1,0:T(8,128)} %fusion.50), calls=%async_computation.3 | async-start | bytes 7864320 | tf_op jit(solution)/shard_map/all_to_all | solution.py:138
  383.5 45.8 %all-to-all-done.3 = f32[8,8,40,384]{3,2,1,0:T(8,128)} async-done(((f32[8,8,40,384]{3,2,1,0:T(8,128)}), f32[8,8,40,384]{3,2,1,0:T(8,128)}, u32[]{:S(2)}, u32[]{:S(2)}) %all-to-all-start.3) | async-done | bytes 3932192 | tf_op jit(solution)/shard_map/all_to_all | solution.py:138
  429.3 4.1 gather_fusion.1
  433.4 1.7 gather.12
  435.1 1.8 fusion.25
  436.9 1.6 copy.251
  (150 shorter events, 5.0 us)
Async XLA Ops:
  0.6 21.5 %copy-start = (f32[16,32]{1,0:T(8,128)S(1)}, f32[16,32]{1,0:T(8,128)}, u32[]{:S(2)}) copy-start(f32[16,32]{1,0:T(8,128)} %param.8) | copy-start | bytes 6148
  15.3 7.0 %copy-start.4 = (s32[640]{0:T(1024)S(1)}, s32[640]{0:T(1024)}, u32[]{:S(2)}) copy-start(s32[640]{0:T(1024)} %param.10) | copy-start | bytes 7684
  15.3 52.6 %all-to-all-start = ((f32[64,40,384]{2,1,0:T(8,128)}), f32[64,40,384]{2,1,0:T(8,128)}, u32[]{:S(2)}, u32[]{:S(2)}) async-start(f32[64,40,384]{2,1,0:T(8,128)} %select_multiply_fusion), calls=%async_computation | async-start | bytes 7864320 | tf_op jit(solution)/shard_map/all_to_all | solution.py:123
  83.2 1.9 copy-start.2
  131.5 8.0 %copy-start.5 = (f32[16,32]{1,0:T(8,128)S(1)}, f32[16,32]{1,0:T(8,128)}, u32[]{:S(2)}) copy-start(f32[16,32]{1,0:T(8,128)} %param.9) | copy-start | bytes 6148
  131.5 65.8 %all-to-all-start.1 = ((f32[16,1,61440]{2,1,0:T(1,128)}), f32[16,1,61440]{2,1,0:T(1,128)}, u32[]{:S(2)}, u32[]{:S(2)}) async-start(f32[16,1,61440]{2,1,0:T(1,128)} %reshape.183), calls=%async_computation.1 | async-start | bytes 7864320 | tf_op jit(solution)/shard_map/all_to_all | solution.py:133
  252.2 1.9 copy-start.3
  375.5 53.8 %all-to-all-start.3 = ((f32[8,8,40,384]{3,2,1,0:T(8,128)}), f32[8,8,40,384]{3,2,1,0:T(8,128)}, u32[]{:S(2)}, u32[]{:S(2)}) async-start(f32[8,8,40,384]{3,2,1,0:T(8,128)} %fusion.50), calls=%async_computation.3 | async-start | bytes 7864320 | tf_op jit(solution)/shard_map/all_to_all | solution.py:138
  433.4 5.2 %copy-start.1 = (f32[16,32]{1,0:T(8,128)S(1)}, f32[16,32]{1,0:T(8,128)}, u32[]{:S(2)}) copy-start(f32[16,32]{1,0:T(8,128)} %param.8) | copy-start | bytes 6148
